TPU v7x, 32 devices: a whole 2x2x4 slice. The times are simulated.
32 devices in a mesh: groups: 2 (over y), chan: 4 (over z), tm: 2 (over x), src: 2 (over core).
Axes of the slice: x: 2, y: 2, z: 4, core: 2. Of those that a mesh axis runs over, the one named last changes fastest.
Arguments:
- record: float32 [8192, 512], P(('groups', 'chan', 'src'), 'tm'), parts along dimension 0, may hold values from -6 to 6
- fir_taps: float32 [4, 128], replicated, may hold values from -0.5 to 0.5
- chan_table: int32 [4096], P(('chan', 'src')), may hold values from 0 to 3
- steering: bfloat16 [32, 256, 128], P(('chan', 'src')), may hold values from -0.375 to 0.375
- pair_block: int32 [64], P(('chan', 'src')), may hold values from 0 to 3
- pair_owner: int32 [64, 1], P(('chan', 'src')), may hold values from 0 to 7; in each aligned block of 8 rows (0 to 7, 8 to 15, ...) at most 2 rows name the same one
- pair_sub: int32 [64], P(('chan', 'src')), may hold values from 0 to 3
- pair_delay: int32 [64], P(('chan', 'src')), may hold values from 1 to 254
- pair_frac: int32 [64], P(('chan', 'src')), may hold values from 0 to 15
Outputs:
- beam: float32 [16384, 512], P(('groups', 'chan', 'src'), 'tm'), parts along dimension 0
There are 2 independent parts, one for each index of `groups`. A program takes and returns all parts, laid end to end along the dimension named above; an argument that names none is the same for every part. Nothing has to cross between parts.
Inputs may be any that keep to these rules, and one draw needn't show every extreme that they name: `pair_owner`: in the rows of one device (aligned blocks of 8 rows) no owner is named more than 2 times, and in every draw some owner is named exactly 2 times in some such block; every owner is named somewhere.
All inputs are finite; a program needn't handle non-finite values.
Results may differ from a plain program's by a relative error of at most 0.0029.
Values may be sent and summed in bfloat16 or wider, within the bound.
A program may use at most 128 MiB of HBM per device.

v0:
```python
import math

import jax
import jax.numpy as jnp
from jax import lax
from jax.sharding import PartitionSpec as P

NFRAC = 16


def shifted_2(value, axis, steps):
    count = lax.axis_size(axis)
    initial, last = (max(0, -steps), min(count, count - steps))
    return lax.ppermute(value, axis, [(source, source + steps) for source in range(initial, last)])


def lagrange(position):
    first = -position * (position - 1.0) * (position - 2.0) / 6.0
    second = (position + 1.0) * (position - 1.0) * (position - 2.0) / 2.0
    third = -(position + 1.0) * position * (position - 2.0) / 2.0
    fourth = (position + 1.0) * position * (position - 1.0) / 6.0
    return jnp.stack([first, second, third, fourth], axis=-1)


def band_filter(window, fir_taps, select, length):
    ntaps = fir_taps.shape[1]
    width = window.shape[1]
    rows_idx = jnp.arange(width, dtype=jnp.int32)[:, None]
    cols_idx = jnp.arange(length, dtype=jnp.int32)[None, :]
    offset = ntaps - 1 + cols_idx - rows_idx
    inside = (offset >= 0) & (offset < ntaps)
    clipped = jnp.clip(offset, 0, ntaps - 1)
    banded = jnp.where(inside[None], jnp.take(fir_taps, clipped, axis=1), 0.0)
    matrix = jnp.transpose(banded, (1, 0, 2)).reshape(width, -1)
    every = jnp.dot(window, matrix, precision=lax.Precision.HIGHEST)
    every = every.reshape(window.shape[0], fir_taps.shape[0], length)
    return jnp.einsum("cm,cml->cl", select, every, precision=lax.Precision.HIGHEST)


def local(
    record, fir_taps, chan_table, steering, pair_block, pair_owner, pair_sub, pair_delay, pair_frac
):
    channel_list, seg = record.shape
    ntaps = fir_taps.shape[1]
    block_rows = steering.shape[2]
    select = (
        chan_table[:, None] == jnp.arange(fir_taps.shape[0], dtype=jnp.int32)[None, :]
    ).astype(jnp.float32)
    before = shifted_2(record, "tm", 1)
    window = jnp.concatenate([before[:, seg - (ntaps - 1) :], record], axis=1)
    filtered_trace = band_filter(window, fir_taps, select, seg)
    after = shifted_2(filtered_trace, "tm", -1)
    extended_trace = jnp.concatenate([filtered_trace, after], axis=1)
    blocks = extended_trace.reshape(channel_list // block_rows, block_rows, 2 * seg)
    weights = lagrange(pair_frac.astype(jnp.float32) / NFRAC)
    pair_count = pair_block.shape[0]
    group = math.gcd(pair_count, 8)

    def one_pair(block_index, delay, weight):
        rows = blocks[block_index]
        window_rows = lax.dynamic_slice_in_dim(rows, delay - 1, seg + 3, 1)
        mixed = weight[0] * window_rows[:, 0:seg] + weight[1] * window_rows[:, 1 : seg + 1]
        mixed = (
            mixed
            + weight[2] * window_rows[:, 2 : seg + 2]
            + weight[3] * window_rows[:, 3 : seg + 3]
        )
        return mixed.astype(jnp.bfloat16)

    def one_group(items):
        return jax.vmap(one_pair)(items[0], items[1], items[2])

    grouped = (
        pair_block.reshape(-1, group),
        pair_delay.reshape(-1, group),
        weights.reshape(-1, group, 4),
    )
    shifted = lax.map(one_group, grouped).reshape(pair_count, block_rows, seg)
    nchan = lax.axis_size("chan")
    nsrc = lax.axis_size("src")
    owners = nchan * nsrc
    capacity = 2 * pair_count // owners
    owner = pair_owner[:, 0]
    hits = (owner[:, None] == jnp.arange(owners, dtype=jnp.int32)[None, :]).astype(jnp.int32)
    earlier = jnp.cumsum(hits, axis=0) - hits
    rank = jnp.sum(earlier * hits, axis=1)
    slot = owner * capacity + rank
    slots = owners * capacity
    match = slot[None, :] == jnp.arange(slots, dtype=jnp.int32)[:, None]
    source_pair = jnp.sum(
        match.astype(jnp.int32) * jnp.arange(pair_count, dtype=jnp.int32)[None, :], axis=1
    )
    live = jnp.any(match, axis=1)
    payload = jnp.where(live[:, None, None], shifted[source_pair], jnp.zeros((), jnp.bfloat16))
    label = jnp.where(live, pair_sub[source_pair], -1).astype(jnp.float32).astype(jnp.bfloat16)
    got, got_label = (
        lax.all_to_all(
            payload.reshape(owners, capacity, block_rows, seg),
            ("chan", "src"),
            split_axis=0,
            concat_axis=0,
            tiled=True,
        ),
        lax.all_to_all(
            label.reshape(owners, capacity),
            ("chan", "src"),
            split_axis=0,
            concat_axis=0,
            tiled=True,
        ),
    )
    flat = got.reshape(slots, block_rows * seg)
    labels = got_label.reshape(slots)
    block_count = steering.shape[0]
    targets = jnp.arange(block_count, dtype=jnp.int32).astype(jnp.float32).astype(jnp.bfloat16)
    pick = (labels[None, :] == targets[:, None]).astype(jnp.bfloat16)
    stacked_sums = jnp.dot(pick, flat, preferred_element_type=jnp.float32).reshape(
        block_count, block_rows, seg
    )
    beam = jnp.einsum(
        "bxc,bct->bxt", steering.astype(jnp.float32), stacked_sums, precision=lax.Precision.HIGHEST
    )
    return beam.reshape(block_count * steering.shape[1], seg)


def solution(mesh):
    in_specs = (
        P(("groups", "chan", "src"), "tm"),
        P(),
        P(("chan", "src")),
        P(("chan", "src"), None, None),
        P(("chan", "src")),
        P(("chan", "src"), None),
        P(("chan", "src")),
        P(("chan", "src")),
        P(("chan", "src")),
    )
    out_specs = P(("groups", "chan", "src"), "tm")
    return jax.shard_map(local, mesh=mesh, in_specs=in_specs, out_specs=out_specs, check_vma=False)
```

profile of v0, /device:TPU:0, one launch (start us, length us, event | category | flops | bytes accessed | tf_op | source)
XLA Modules:
  0.0 289.2 jit_solution(188469917775165775)
XLA Ops:
  0.0 0.0 copy-start
  0.0 0.0 copy-start.2
  0.0 0.8 fusion.30
  0.8 0.8 select_reduce_fusion.1
  1.7 0.7 multiply_add_fusion
  2.3 0.1 fusion.29
  2.4 0.1 select_reduce_fusion
  2.5 1.3 gather_fusion
  3.8 0.7 convert_element_type.62
  4.5 6.4 %all-to-all-start = ((bf16[8,1,2]{2,1,0:T(2,128)(2,1)}), bf16[8,1,2]{2,1,0:T(2,128)(2,1)S(1)}, u32[]{:S(2)}, u32[]{:S(2)}) async-start(bf16[8,1,2]{2,1,0:T(2,128)(2,1)} %convert_element_type.62), calls=%async_computation | async-start | bytes 8192 | tf_op jit(solution)/shard_map/all_to_all | solution.py:104
  10.9 3.4 %collective-permute-start = (f32[512,256]{1,0:T(8,128)}, f32[512,256]{1,0:T(8,128)S(1)}, u32[]{:S(2)}, u32[]{:S(2)}) collective-permute-start(f32[512,256]{1,0:T(8,128)} %param.9), channel_id=1, source_target_pairs={{0,2},{1,3},{4,6},{5,7},{8,10},{9,11},{12,14},{13,15},{16,18},{17,... | collective-permute-start | bytes 1572872 | tf_op jit(solution)/shard_map/ppermute | solution.py:14
  14.3 0.1 compare_select_fusion
  14.5 0.1 pad_clamp_fusion
  14.5 0.0 copy-done.2
  14.5 0.1 copy.30
  14.6 180.3 %gather_fusion.1 = f32[98048,4]{1,0:T(8,128)} fusion(f32[4,128]{0,1:T(8,128)S(1)} %copy.30, s32[98304]{0:T(1024)S(1)} %pad_clamp_fusion), kind=kCustom, calls=%fused_computation.1 | custom fusion | bytes 3529728 | tf_op jit(solution)/shard_map/jit(_take)/gather | solution.py:33
  194.9 0.0 copy-start.3
  194.9 0.0 copy-start.1
  194.9 28.0 %copy.31 = f32[383,256,4]{0,1,2:T(8,128)S(1)} copy(f32[383,256,4]{2,1,0:T(8,128)} %bitcast.53) | data formatting | bytes 3137536 | tf_op jit(solution)/shard_map/jit(_take)/gather | solution.py:33
  223.0 0.0 copy-done.3
  223.0 0.1 fusion.28
  223.1 0.3 fusion.26
  223.4 0.0 collective-permute-done
  223.4 0.1 slice.46
  223.6 0.0 copy-done.1
  223.6 3.7 %fusion.2 = f32[512,4,256]{2,0,1:T(8,128)S(1)} fusion(f32[383,256,4]{0,1,2:T(8,128)S(1)} %copy.31, f32[512,256]{1,0:T(8,128)S(1)} %copy-done.1, f32[512,127]{1,0:T(8,128)S(1)} %slice.46, pred[383,256]{0,1:T(8,128)(4,1)S(1)} %get-tuple-element.16, pred[383,256]{0,1:T(8,128)(4,1)S(1)} %get-tuple-element.15), kind=kOutput, calls=%fused_computation.7 | convolution fusion | flops 2410608128 | bytes 4646400 | tf_op jit(solution)/shard_map/dot_general | solution.py:35
  227.3 0.0 copy-start.5
  227.3 0.0 copy-start.6
  227.3 0.0 copy-start.4
  227.3 3.5 %fusion = f32[512,1,256]{2,1,0:T(1,128)S(1)} fusion(f32[512,4,256]{2,0,1:T(8,128)S(1)} %fusion.2, pred[512,4,1]{1,0,2:T(32,128)(4,1)S(1)} %fusion.28), kind=kOutput, calls=%fused_computation.5 | convolution fusion | flops 6291456 | bytes 2623488 | tf_op jit(solution)/shard_map/cm,cml->cl/dot_general | solution.py:37
  230.9 1.5 collective-permute-start.1
  232.4 0.0 copy-done.5
  232.4 0.1 broadcast_in_dim.66
  232.5 0.0 copy-done.6
  232.5 0.0 copy-done.4
  232.5 14.3 %collective-permute-done.1 = f32[512,256]{1,0:T(8,128)S(1)} collective-permute-done((f32[512,256]{1,0:T(8,128)S(1)}, f32[512,256]{1,0:T(8,128)S(1)}, u32[]{:S(2)}, u32[]{:S(2)}) %collective-permute-start.1) | collective-permute-done | bytes 524320 | tf_op jit(solution)/shard_map/ppermute | solution.py:14
  246.8 0.1 pad_maximum_fusion
  247.0 2.0 gather_fusion.2
  249.0 2.1 copy.32
  251.1 2.1 gather_fusion.4
  253.2 0.3 fusion.10
  253.6 0.3 copy.33
  253.9 0.6 gather_fusion.3
  254.5 1.1 broadcast_select_fusion
  255.6 0.0 all-to-all-done
  255.6 4.7 %all-to-all-start.1 = ((bf16[8,2,128,256]{3,2,1,0:T(8,128)(2,1)}), bf16[8,2,128,256]{3,2,1,0:T(8,128)(2,1)S(1)}, u32[]{:S(2)}, u32[]{:S(2)}) async-start(bf16[8,2,128,256]{3,2,1,0:T(8,128)(2,1)} %broadcast_select_fusion), calls=%async_computation.1 | async-start | bytes 2097152 | tf_op jit(solution)/shard_map/all_to_all | solution.py:97
  260.4 0.1 eq.60
  260.5 26.4 %all-to-all-done.1 = bf16[8,2,128,256]{3,2,1,0:T(8,128)(2,1)S(1)} async-done(((bf16[8,2,128,256]{3,2,1,0:T(8,128)(2,1)}), bf16[8,2,128,256]{3,2,1,0:T(8,128)(2,1)S(1)}, u32[]{:S(2)}, u32[]{:S(2)}) %all-to-all-start.1) | async-done | bytes 1048608 | tf_op jit(solution)/shard_map/all_to_all | solution.py:97
  286.9 0.7 fusion.6
  287.6 0.0 copy-done
  287.6 1.6 fusion.20
  (12 shorter events, 0.2 us)
Async XLA Ops:
  0.0 287.6 %copy-start = (bf16[4,256,128]{2,1,0:T(8,128)(2,1)S(1)}, bf16[4,256,128]{2,1,0:T(8,128)(2,1)}, u32[]{:S(2)}) copy-start(bf16[4,256,128]{2,1,0:T(8,128)(2,1)} %param.12) | copy-start | bytes 786436
  0.0 14.5 %copy-start.2 = (f32[4,128]{1,0:T(4,128)S(1)}, f32[4,128]{1,0:T(4,128)}, u32[]{:S(2)}) copy-start(f32[4,128]{1,0:T(4,128)} %param.10) | copy-start | bytes 6148
  4.5 251.1 %all-to-all-start = ((bf16[8,1,2]{2,1,0:T(2,128)(2,1)}), bf16[8,1,2]{2,1,0:T(2,128)(2,1)S(1)}, u32[]{:S(2)}, u32[]{:S(2)}) async-start(bf16[8,1,2]{2,1,0:T(2,128)(2,1)} %convert_element_type.62), calls=%async_computation | async-start | bytes 8192 | tf_op jit(solution)/shard_map/all_to_all | solution.py:104
  10.9 212.6 %collective-permute-start = (f32[512,256]{1,0:T(8,128)}, f32[512,256]{1,0:T(8,128)S(1)}, u32[]{:S(2)}, u32[]{:S(2)}) collective-permute-start(f32[512,256]{1,0:T(8,128)} %param.9), channel_id=1, source_target_pairs={{0,2},{1,3},{4,6},{5,7},{8,10},{9,11},{12,14},{13,15},{16,18},{17,... | collective-permute-start | bytes 1572872 | tf_op jit(solution)/shard_map/ppermute | solution.py:14
  194.9 28.0 %copy-start.3 = (s32[512]{0:T(512)S(1)}, s32[512]{0:T(512)}, u32[]{:S(2)}) copy-start(s32[512]{0:T(512)} %param.11) | copy-start | bytes 6148
  194.9 28.6 %copy-start.1 = (f32[512,256]{1,0:T(8,128)S(1)}, f32[512,256]{1,0:T(8,128)}, u32[]{:S(2)}) copy-start(f32[512,256]{1,0:T(8,128)} %param.9) | copy-start | bytes 1572868
  227.3 5.1 %copy-start.5 = (s32[8]{0:T(128)S(1)}, s32[8]{0:T(128)}, u32[]{:S(2)}) copy-start(s32[8]{0:T(128)} %param.13) | copy-start | bytes 100
  227.3 5.2 %copy-start.6 = (s32[8]{0:T(128)S(1)}, s32[8]{0:T(128)}, u32[]{:S(2)}) copy-start(s32[8]{0:T(128)} %param.16) | copy-start | bytes 100
  227.3 5.2 %copy-start.4 = (s32[8]{0:T(128)S(1)}, s32[8]{0:T(128)}, u32[]{:S(2)}) copy-start(s32[8]{0:T(128)} %param.17) | copy-start | bytes 100
  230.9 15.9 %collective-permute-start.1 = (f32[512,256]{1,0:T(8,128)S(1)}, f32[512,256]{1,0:T(8,128)S(1)}, u32[]{:S(2)}, u32[]{:S(2)}) collective-permute-start(f32[512,256]{1,0:T(8,128)S(1)} %bitcast.57), channel_id=1, source_target_pairs={{2,0},{3,1},{6,4},{7,5},{10,8},{11,9},{14,12},{15,13},{18,16},{19,... | collective-permute-start | bytes 1572872 | tf_op jit(solution)/shard_map/ppermute | solution.py:14
  255.6 31.3 %all-to-all-start.1 = ((bf16[8,2,128,256]{3,2,1,0:T(8,128)(2,1)}), bf16[8,2,128,256]{3,2,1,0:T(8,128)(2,1)S(1)}, u32[]{:S(2)}, u32[]{:S(2)}) async-start(bf16[8,2,128,256]{3,2,1,0:T(8,128)(2,1)} %broadcast_select_fusion), calls=%async_computation.1 | async-start | bytes 2097152 | tf_op jit(solution)/shard_map/all_to_all | solution.py:97
where the time goes:
time: 290 us; the launch traced here: 289 us
  local copies, waits for them, and re-layouts  218 us (75%)
  waiting for transfers between devices  40.8 us (14%)
  starting transfers between devices  16 us (6%)
  matrix products  9.49 us (3%)
  other arithmetic  4.78 us (2%)
    gather x2, local copies, waits for them, and re-layouts, band_filter(): banded = jnp.where(inside[None], jnp.take(fir_taps, clipped, axis=1), 0.0)  208 us
    all_to_all x1, waiting for transfers between devices, local(): lax.all_to_all(payload.reshape(owners, capacity, block_rows, seg), ('chan...  26.4 us
    ppermute x2, waiting for transfers between devices, shifted_2(): lax.ppermute(value, axis, [(source, source + steps) for source in range(i...  14.3 us
    all_to_all x1, starting transfers between devices, local(): lax.all_to_all(label.reshape(owners, capacity), ('chan', 'src'), split_ax...  6.35 us
  transfers between devices with their start and end apart: 4, of which 2 were waited for; matrix products, arithmetic and copies ran while one was open for 78% of the time, Pallas kernels for 0%

commit v1 on v0

v1 whole, which is shorter than its diff:
```python
import functools

import jax
import jax.numpy as jnp
from jax import lax
from jax.experimental import pallas as pl
from jax.experimental.pallas import tpu as pltpu
from jax.sharding import PartitionSpec as P

NFRAC = 16
GROUPS = 4
MESH = pl.DeviceIdType.MESH


def split(value):
    high = value.astype(jnp.bfloat16)
    return high, (value - high.astype(jnp.float32)).astype(jnp.bfloat16)


def mm(a, b):
    return jnp.dot(a, b, preferred_element_type=jnp.float32)


def kernel(
    dims,
    block_ref,
    owner_ref,
    sub_ref,
    delay_ref,
    frac_ref,
    record,
    taps_ref,
    table_ref,
    steer_ref,
    beam_ref,
    prev,
    after,
    band_hi,
    band_lo,
    tab,
    filt,
    shifted,
    out_slots,
    in_slots,
    out_label,
    in_label,
    sums,
    slot_pair,
    prev_send,
    prev_recv,
    after_send,
    after_recv,
    slot_send,
    slot_recv,
    label_send,
    label_recv,
):
    nchan, nsrc, ntm = dims
    owners = nchan * nsrc
    blocks, block_rows, seg = record.shape
    ntab, ntaps = taps_ref.shape
    pairs = block_ref.shape[0]
    cap = out_slots.shape[1]
    targets = steer_ref.shape[0]
    points = steer_ref.shape[1]
    step_rows = block_rows // GROUPS
    rows = blocks * step_rows
    me = lax.axis_index("chan") * nsrc + lax.axis_index("src")
    tm = lax.axis_index("tm")

    def place(owner):
        return {"chan": owner // nsrc, "src": owner % nsrc}

    barrier = pltpu.get_barrier_semaphore()

    @pl.when(tm > 0)
    def _():
        pl.semaphore_signal(barrier, inc=1, device_id={"tm": tm - 1}, device_id_type=MESH)

    @pl.when(tm < ntm - 1)
    def _():
        pl.semaphore_signal(barrier, inc=1, device_id={"tm": tm + 1}, device_id_type=MESH)

    def greet(i, carry):
        pl.semaphore_signal(
            barrier, inc=1, device_id=place((me + i) % owners), device_id_type=MESH
        )
        return carry

    lax.fori_loop(1, owners, greet, 0)

    for m in range(ntab):
        row = jnp.concatenate([taps_ref[m : m + 1, :], jnp.zeros((1, ntaps), jnp.float32)], axis=1)
        full = jnp.broadcast_to(row, (2 * ntaps, 2 * ntaps))
        rolled = pltpu.roll(full, ntaps, 1, stride=1, stride_axis=0)[:, :ntaps]
        high, low = split(rolled)
        band_hi[:, m * ntaps : (m + 1) * ntaps] = high
        band_lo[:, m * ntaps : (m + 1) * ntaps] = low

    @pl.when(tm == 0)
    def _():
        prev[...] = jnp.zeros_like(prev)

    @pl.when(tm == ntm - 1)
    def _():
        after[...] = jnp.zeros_like(after)

    pl.semaphore_wait(
        barrier,
        owners - 1 + jnp.where(tm > 0, 1, 0) + jnp.where(tm < ntm - 1, 1, 0),
    )

    def part(r):
        return pl.ds(pl.multiple_of(r * step_rows, step_rows), step_rows)

    def to_prev(r):
        return pltpu.make_async_remote_copy(
            src_ref=record.at[:, part(r), pl.ds(seg - ntaps, ntaps)],
            dst_ref=prev.at[:, part(r), :],
            send_sem=prev_send.at[r],
            recv_sem=prev_recv.at[r],
            device_id={"tm": tm + 1},
            device_id_type=MESH,
        )

    def to_after(r):
        return pltpu.make_async_remote_copy(
            src_ref=record.at[:, part(r), :],
            dst_ref=after.at[:, part(r), :],
            send_sem=after_send.at[r],
            recv_sem=after_recv.at[r],
            device_id={"tm": tm - 1},
            device_id_type=MESH,
        )

    def slots_to(r, other, landing):
        return pltpu.make_async_remote_copy(
            src_ref=out_slots.at[other, :, part(r), :],
            dst_ref=in_slots.at[landing, :, part(r), :],
            send_sem=slot_send.at[r, other],
            recv_sem=slot_recv.at[r, landing],
            device_id=place(other),
            device_id_type=MESH,
        )

    def label_to(other, landing):
        return pltpu.make_async_remote_copy(
            src_ref=out_label.at[other],
            dst_ref=in_label.at[landing],
            send_sem=label_send.at[other],
            recv_sem=label_recv.at[landing],
            device_id=place(other),
            device_id_type=MESH,
        )

    for r in range(GROUPS):

        @pl.when(tm > 0)
        def _():
            to_after(r).start()

        @pl.when(tm < ntm - 1)
        def _():
            to_prev(r).start()

    for g in range(blocks):
        tab[g] = jnp.broadcast_to(table_ref[g : g + 1, :], (block_rows, block_rows)).T

    def slots_of(owner, carry):
        def look(p, found):
            hit = owner_ref[p] == owner
            count = found[0]
            named = [
                jnp.where(jnp.logical_and(hit, count == k), p, found[1 + k]) for k in range(cap)
            ]
            return (count + jnp.where(hit, 1, 0), *named)

        found = lax.fori_loop(0, pairs, look, (0,) + (-1,) * cap, unroll=min(pairs, 8))
        line = lax.broadcasted_iota(jnp.int32, out_label.shape[1:], 0)
        labels = jnp.full(out_label.shape[1:], -1.0, jnp.float32)
        for k in range(cap):
            pair = jnp.maximum(found[1 + k], 0)
            slot_pair[owner * cap + k] = pair
            name = jnp.where(found[1 + k] >= 0, sub_ref[pair], -1).astype(jnp.float32)
            labels = jnp.where(line == k, name, labels)
        out_label[owner] = labels
        return carry

    lax.fori_loop(0, owners, slots_of, 0)

    def send_label(i, carry):
        label_to((me + i) % owners, me).start()
        return carry

    lax.fori_loop(1, owners, send_label, 0)

    def produce(r, carry):
        @pl.when(tm > 0)
        def _():
            to_prev(r).wait_recv()

        @pl.when(tm < ntm - 1)
        def _():
            to_after(r).wait_recv()

        window = jnp.concatenate(
            [
                prev[:, part(r), :].reshape(rows, ntaps),
                record[:, part(r), :].reshape(rows, seg),
                after[:, part(r), :].reshape(rows, seg),
            ],
            axis=1,
        )
        high, low = split(window)
        steps = 2 * seg // ntaps
        lhs_hi = jnp.concatenate([high[:, j * ntaps : (j + 2) * ntaps] for j in range(steps)], axis=0)
        lhs_lo = jnp.concatenate([low[:, j * ntaps : (j + 2) * ntaps] for j in range(steps)], axis=0)
        every = mm(lhs_lo, band_hi[...]) + mm(lhs_hi, band_lo[...]) + mm(lhs_hi, band_hi[...])
        which = tab[:, part(r), :].reshape(rows, block_rows)
        inside = jnp.where(tm < ntm - 1, 1.0, 0.0)
        for j in range(steps):
            own = every[j * rows : (j + 1) * rows]
            value = own[:, :ntaps]
            for m in range(1, ntab):
                value = jnp.where(which == m, own[:, m * ntaps : (m + 1) * ntaps], value)
            if j >= seg // ntaps:
                value = value * inside
            filt[:, :, j * ntaps : (j + 1) * ntaps] = value.reshape(blocks, step_rows, ntaps)

        def one_pair(p, c):
            mu = jnp.full((1, seg), frac_ref[p].astype(jnp.float32)) / NFRAC
            first = -mu * (mu - 1.0) * (mu - 2.0) / 6.0
            second = (mu + 1.0) * (mu - 1.0) * (mu - 2.0) / 2.0
            third = -(mu + 1.0) * mu * (mu - 2.0) / 2.0
            fourth = (mu + 1.0) * mu * (mu - 1.0) / 6.0
            source = filt[block_ref[p]]
            base = pltpu.roll(source, 2 * seg - (delay_ref[p] - 1), 1)
            mixed = first * base[:, :seg]
            mixed = mixed + second * pltpu.roll(base, 2 * seg - 1, 1)[:, :seg]
            mixed = mixed + third * pltpu.roll(base, 2 * seg - 2, 1)[:, :seg]
            mixed = mixed + fourth * pltpu.roll(base, 2 * seg - 3, 1)[:, :seg]
            shifted[p] = mixed.astype(jnp.bfloat16)
            return c

        lax.fori_loop(0, pairs, one_pair, 0, unroll=min(pairs, 4))

        def ship(i, c):
            other = (me + owners // 2 + i) % owners
            for k in range(cap):
                out_slots[other, k, part(r), :] = shifted[slot_pair[other * cap + k]]

            @pl.when(other != me)
            def _():
                slots_to(r, other, me).start()

            return c

        lax.fori_loop(0, owners, ship, 0)
        return carry

    lax.fori_loop(0, GROUPS, produce, 0)

    def wait_label(i, carry):
        source = (me + i) % owners
        label_to(source, source).wait_recv()
        return carry

    lax.fori_loop(1, owners, wait_label, 0)

    def add(total, values, labels):
        for k in range(cap):
            name = jnp.concatenate([labels[k : k + 1, :]] * (seg // labels.shape[1]), axis=1)
            value = values[k].astype(jnp.float32)
            total = [
                total[b] + value * jnp.where(name == float(b), 1.0, 0.0) for b in range(targets)
            ]
        return total

    def gather(r, carry):
        total = [jnp.zeros((step_rows, seg), jnp.float32)] * targets
        total = add(total, out_slots[me, :, part(r), :], out_label[me])

        def one_source(i, running):
            source = (me + i) % owners
            slots_to(r, source, source).wait_recv()
            return tuple(add(list(running), in_slots[source, :, part(r), :], in_label[source]))

        total = lax.fori_loop(1, owners, one_source, tuple(total))
        for b in range(targets):
            sums[b, part(r), :] = total[b]
        return carry

    lax.fori_loop(0, GROUPS, gather, 0)

    for b in range(targets):
        high, low = split(sums[b])
        beam_ref[b * points : (b + 1) * points, :] = mm(steer_ref[b], high) + mm(steer_ref[b], low)

    def finish(i, carry):
        other = (me + i) % owners
        label_to(other, me).wait_send()
        for r in range(GROUPS):
            slots_to(r, other, me).wait_send()
        return carry

    lax.fori_loop(1, owners, finish, 0)
    for r in range(GROUPS):

        @pl.when(tm > 0)
        def _():
            to_after(r).wait_send()

        @pl.when(tm < ntm - 1)
        def _():
            to_prev(r).wait_send()


def solution(mesh):
    nchan, nsrc, ntm = mesh.shape["chan"], mesh.shape["src"], mesh.shape["tm"]
    owners = nchan * nsrc

    def local(
        record, fir_taps, chan_table, steering, pair_block, pair_owner, pair_sub, pair_delay, pair_frac
    ):
        channels, seg = record.shape
        ntab, ntaps = fir_taps.shape
        targets, points, block_rows = steering.shape
        blocks = channels // block_rows
        pairs = pair_block.shape[0]
        cap = 2 * pairs // owners
        step_rows = block_rows // GROUPS
        smem = pl.BlockSpec(memory_space=pltpu.SMEM)
        vmem = pl.BlockSpec(memory_space=pltpu.VMEM)
        dma = pltpu.SemaphoreType.DMA
        return pl.pallas_call(
            functools.partial(kernel, (nchan, nsrc, ntm)),
            out_shape=jax.ShapeDtypeStruct((targets * points, seg), jnp.float32),
            in_specs=[smem] * 5 + [vmem] * 4,
            out_specs=vmem,
            scratch_shapes=[
                pltpu.VMEM((blocks, block_rows, ntaps), jnp.float32),
                pltpu.VMEM((blocks, block_rows, seg), jnp.float32),
                pltpu.VMEM((2 * ntaps, ntab * ntaps), jnp.bfloat16),
                pltpu.VMEM((2 * ntaps, ntab * ntaps), jnp.bfloat16),
                pltpu.VMEM((blocks, block_rows, block_rows), jnp.int32),
                pltpu.VMEM((blocks, step_rows, 2 * seg), jnp.float32),
                pltpu.VMEM((pairs, step_rows, seg), jnp.bfloat16),
                pltpu.VMEM((owners, cap, block_rows, seg), jnp.bfloat16),
                pltpu.VMEM((owners, cap, block_rows, seg), jnp.bfloat16),
                pltpu.VMEM((owners, 8, 128), jnp.float32),
                pltpu.VMEM((owners, 8, 128), jnp.float32),
                pltpu.VMEM((targets, block_rows, seg), jnp.float32),
                pltpu.SMEM((owners * cap,), jnp.int32),
                dma((GROUPS,)),
                dma((GROUPS,)),
                dma((GROUPS,)),
                dma((GROUPS,)),
                dma((GROUPS, owners)),
                dma((GROUPS, owners)),
                dma((owners,)),
                dma((owners,)),
            ],
            compiler_params=pltpu.CompilerParams(collective_id=0, has_side_effects=True),
        )(
            pair_block,
            pair_owner.reshape(pairs),
            pair_sub,
            pair_delay,
            pair_frac,
            record.reshape(blocks, block_rows, seg),
            fir_taps,
            chan_table.reshape(blocks, block_rows),
            steering,
        )

    in_specs = (
        P(("groups", "chan", "src"), "tm"),
        P(),
        P(("chan", "src")),
        P(("chan", "src"), None, None),
        P(("chan", "src")),
        P(("chan", "src"), None),
        P(("chan", "src")),
        P(("chan", "src")),
        P(("chan", "src")),
    )
    out_specs = P(("groups", "chan", "src"), "tm")
    return jax.shard_map(local, mesh=mesh, in_specs=in_specs, out_specs=out_specs, check_vma=False)
```

time: 290 us -> 40.6 us (0.14)
  local copies, waits for them, and re-layouts: 218 us -> 2.26 us
  waiting for transfers between devices: 40.8 us -> 0 us
  Pallas kernels: 0 us -> 38.1 us
  starting transfers between devices: 16 us -> 0 us
  matrix products: 9.49 us -> 0 us
  other arithmetic: 4.78 us -> 0 us
    gather x7 -> x0, local copies, waits for them, and re-layouts: 216 us -> none  [the longest x2 208 us: band_filter(): banded = jnp.where(inside[None], jnp.take(fir_taps, clipped, axis=1), 0.0)]
    pallas_call x0 -> x1, Pallas kernels: none -> 38.1 us  [local(): pl.pallas_call(functools.partial(kernel, (nchan, nsrc, ntm)), out_shape=j...]
    all_to_all x2 -> x0, waiting for transfers between devices: 26.4 us -> none  [the longest x1 26.4 us: local(): lax.all_to_all(payload.reshape(owners, capacity, block_rows, seg), ('chan...]
    ppermute x2 -> x0, waiting for transfers between devices: 14.3 us -> none  [shifted_2(): lax.ppermute(value, axis, [(source, source + steps) for source in range(i...]
    all_to_all x2 -> x0, starting transfers between devices: 11.1 us -> none  [the longest x1 6.35 us: local(): lax.all_to_all(label.reshape(owners, capacity), ('chan', 'src'), split_ax...]
    dot_general x4 -> x0, matrix products: 9.49 us -> none  [the longest x1 3.7 us: band_filter(): every = jnp.dot(window, matrix, precision=lax.Precision.HIGHEST)]
    ppermute x2 -> x0, starting transfers between devices: 4.89 us -> none  [shifted_2(): lax.ppermute(value, axis, [(source, source + steps) for source in range(i...]
  transfers between devices with their start and end apart: 4 -> 0, of which waited for: 2 -> 0; matrix products, arithmetic and copies ran while one was open for 78% -> 0% of each run, Pallas kernels for 0% -> 0%
where the time goes in v1:
time: 40.6 us; the launch traced here: 40.4 us
  Pallas kernels  38.1 us (94%)
  local copies, waits for them, and re-layouts  2.26 us (6%)
    pallas_call x1, Pallas kernels, local(): pl.pallas_call(functools.partial(kernel, (nchan, nsrc, ntm)), out_shape=j...  38.1 us
    unnamed x1, local copies, waits for them, and re-layouts  2.26 us

profile of v1, /device:TPU:0, one launch (start us, length us, event | category | flops | bytes accessed | tf_op | source)
XLA Modules:
  0.0 40.4 jit_solution(13542670218181038458)
XLA Ops:
  0.0 38.1 %shard_map.91 = f32[1024,256]{1,0:T(8,128)} custom-call(s32[8]{0:T(128)} %block_ref.1, s32[8]{0:T(128)} %bitcast.5, s32[8]{0:T(128)} %sub_ref.1, s32[8]{0:T(128)} %delay_ref.1, s32[8]{0:T(128)} %frac_ref.1, f32[4,128,256]{2,1,0:T(8,128)} %bitcast.3, f32[4,128]{1,0:T(4,128)} %taps_ref.1, s32[4,128]{1,0:T(4,128)} %bitcast.4, bf16[4,256,128]{2,1,0:T(8,128)(2,1)} %steer_ref.1), custom_call_target="tpu_custom_call" | custom-call | tf_op jit(solution)/shard_map/pallas_call | solution.py:335
  38.1 2.3 %copy.11 = f32[1024,256]{1,0:T(8,128)} copy(f32[1024,256]{1,0:T(8,128)} %shard_map.91) | data formatting | bytes 2097152

commit v2 on v1

--- a/solution.py
+++ b/solution.py
@@ -9,6 +9,9 @@
 
 NFRAC = 16
 GROUPS = 4
+PARTS = 8
+LAG = 2
+MORE = 1
 MESH = pl.DeviceIdType.MESH
 
 
@@ -89,13 +92,7 @@
 
     lax.fori_loop(1, owners, greet, 0)
 
-    for m in range(ntab):
-        row = jnp.concatenate([taps_ref[m : m + 1, :], jnp.zeros((1, ntaps), jnp.float32)], axis=1)
-        full = jnp.broadcast_to(row, (2 * ntaps, 2 * ntaps))
-        rolled = pltpu.roll(full, ntaps, 1, stride=1, stride_axis=0)[:, :ntaps]
-        high, low = split(rolled)
-        band_hi[:, m * ntaps : (m + 1) * ntaps] = high
-        band_lo[:, m * ntaps : (m + 1) * ntaps] = low
+    build_band(taps_ref, band_hi, band_lo)
 
     @pl.when(tm == 0)
     def _():
@@ -211,35 +208,12 @@
             ],
             axis=1,
         )
-        high, low = split(window)
-        steps = 2 * seg // ntaps
-        lhs_hi = jnp.concatenate([high[:, j * ntaps : (j + 2) * ntaps] for j in range(steps)], axis=0)
-        lhs_lo = jnp.concatenate([low[:, j * ntaps : (j + 2) * ntaps] for j in range(steps)], axis=0)
-        every = mm(lhs_lo, band_hi[...]) + mm(lhs_hi, band_lo[...]) + mm(lhs_hi, band_hi[...])
+        inside = jnp.where(tm < ntm - 1, 1.0, 0.0)
         which = tab[:, part(r), :].reshape(rows, block_rows)
-        inside = jnp.where(tm < ntm - 1, 1.0, 0.0)
-        for j in range(steps):
-            own = every[j * rows : (j + 1) * rows]
-            value = own[:, :ntaps]
-            for m in range(1, ntab):
-                value = jnp.where(which == m, own[:, m * ntaps : (m + 1) * ntaps], value)
-            if j >= seg // ntaps:
-                value = value * inside
-            filt[:, :, j * ntaps : (j + 1) * ntaps] = value.reshape(blocks, step_rows, ntaps)
+        band_filter(window, band_hi, band_lo, which, inside, seg, ntab, filt)
 
         def one_pair(p, c):
-            mu = jnp.full((1, seg), frac_ref[p].astype(jnp.float32)) / NFRAC
-            first = -mu * (mu - 1.0) * (mu - 2.0) / 6.0
-            second = (mu + 1.0) * (mu - 1.0) * (mu - 2.0) / 2.0
-            third = -(mu + 1.0) * mu * (mu - 2.0) / 2.0
-            fourth = (mu + 1.0) * mu * (mu - 1.0) / 6.0
-            source = filt[block_ref[p]]
-            base = pltpu.roll(source, 2 * seg - (delay_ref[p] - 1), 1)
-            mixed = first * base[:, :seg]
-            mixed = mixed + second * pltpu.roll(base, 2 * seg - 1, 1)[:, :seg]
-            mixed = mixed + third * pltpu.roll(base, 2 * seg - 2, 1)[:, :seg]
-            mixed = mixed + fourth * pltpu.roll(base, 2 * seg - 3, 1)[:, :seg]
-            shifted[p] = mixed.astype(jnp.bfloat16)
+            shifted[p] = shift_pair(filt[block_ref[p]], delay_ref[p], frac_ref[p], seg)
             return c
 
         lax.fori_loop(0, pairs, one_pair, 0, unroll=min(pairs, 4))
@@ -313,6 +287,459 @@
         @pl.when(tm < ntm - 1)
         def _():
             to_prev(r).wait_send()
+
+
+def copy_to(source, target, send, receive, place):
+    return pltpu.make_async_remote_copy(
+        src_ref=source,
+        dst_ref=target,
+        send_sem=send,
+        recv_sem=receive,
+        device_id=place,
+        device_id_type=MESH,
+    )
+
+
+def line_kernel(
+    dims,
+    block_ref,
+    owner_ref,
+    sub_ref,
+    delay_ref,
+    frac_ref,
+    record,
+    taps_ref,
+    table_ref,
+    steer_ref,
+    beam_ref,
+    prev,
+    after,
+    band_hi,
+    band_lo,
+    tab,
+    filt,
+    shifted,
+    held,
+    names,
+    out_slots,
+    in_slots,
+    out_label,
+    in_label,
+    out_dense,
+    in_dense,
+    sums,
+    slot_pair,
+    prev_send,
+    prev_recv,
+    after_send,
+    after_recv,
+    held_send,
+    held_recv,
+    name_send,
+    name_recv,
+    slot_send,
+    slot_recv,
+    label_send,
+    label_recv,
+    dense_send,
+    dense_recv,
+):
+    nchan, nsrc, ntm = dims
+    blocks, block_rows, seg = record.shape
+    ntab, ntaps = taps_ref.shape
+    pairs = block_ref.shape[0]
+    cap = out_slots.shape[1]
+    targets = steer_ref.shape[0]
+    points = steer_ref.shape[1]
+    step_rows = block_rows // PARTS
+    rows = blocks * step_rows
+    chip = lax.axis_index("chan")
+    core = lax.axis_index("src")
+    mate = 1 - core
+    tm = lax.axis_index("tm")
+    me = chip * nsrc + core
+    middle = jnp.logical_and(chip > 0, chip < nchan - 1)
+    ending = jnp.logical_or(chip == 0, chip == nchan - 1)
+    low_half = chip < nchan // 2
+    outer = jnp.where(low_half, 0, nchan - 1)
+    inner = jnp.where(low_half, 1, nchan - 2)
+    other = nchan - 1 - inner
+    far = nchan - 1 - outer
+
+    barrier = pltpu.get_barrier_semaphore()
+
+    def greet(place):
+        pl.semaphore_signal(barrier, inc=1, device_id=place, device_id_type=MESH)
+
+    @pl.when(tm > 0)
+    def _():
+        greet({"tm": tm - 1})
+
+    @pl.when(tm < ntm - 1)
+    def _():
+        greet({"tm": tm + 1})
+
+    greet({"src": mate})
+
+    @pl.when(middle)
+    def _():
+        greet({"chan": far, "src": core})
+        greet({"chan": other, "src": core})
+        greet({"chan": outer, "src": core})
+        greet({"chan": outer, "src": mate})
+
+    @pl.when(ending)
+    def _():
+        greet({"chan": other, "src": core})
+        greet({"chan": inner, "src": core})
+        greet({"chan": inner, "src": mate})
+
+    build_band(taps_ref, band_hi, band_lo)
+
+    @pl.when(tm == 0)
+    def _():
+        prev[...] = jnp.zeros_like(prev)
+
+    @pl.when(tm == ntm - 1)
+    def _():
+        after[...] = jnp.zeros_like(after)
+
+    pl.semaphore_wait(
+        barrier,
+        jnp.where(middle, 5, 4) + jnp.where(tm > 0, 1, 0) + jnp.where(tm < ntm - 1, 1, 0),
+    )
+
+    def part(r):
+        return pl.ds(pl.multiple_of(r * step_rows, step_rows), step_rows)
+
+    def to_prev(r):
+        return copy_to(
+            record.at[:, part(r), pl.ds(seg - ntaps, ntaps)],
+            prev.at[:, part(r), :],
+            prev_send.at[r],
+            prev_recv.at[r],
+            {"tm": tm + 1},
+        )
+
+    def to_after(r):
+        return copy_to(
+            record.at[:, part(r), :],
+            after.at[:, part(r), :],
+            after_send.at[r],
+            after_recv.at[r],
+            {"tm": tm - 1},
+        )
+
+    def held_to(kind, r, place):
+        source = 2 if kind == 3 else 0
+        return copy_to(
+            held.at[pl.ds(source * pairs, pairs), part(r), :],
+            held.at[pl.ds(kind * pairs, pairs), part(r), :],
+            held_send.at[kind, r],
+            held_recv.at[kind, r],
+            place,
+        )
+
+    def name_to(kind, place):
+        return copy_to(
+            names.at[0], names.at[kind], name_send.at[kind], name_recv.at[kind], place
+        )
+
+    def slots_to(k, r, landing):
+        return copy_to(
+            out_slots.at[k, :, part(r), :],
+            in_slots.at[landing, :, part(r), :],
+            slot_send.at[k, r],
+            slot_recv.at[landing, r],
+            {"chan": outer, "src": k},
+        )
+
+    def label_to(k, landing):
+        return copy_to(
+            out_label.at[k],
+            in_label.at[landing],
+            label_send.at[k],
+            label_recv.at[landing],
+            {"chan": outer, "src": k},
+        )
+
+    def dense_to(k, r):
+        return copy_to(
+            out_dense.at[k, :, part(r), :],
+            in_dense.at[:, part(r), :],
+            dense_send.at[k, r],
+            dense_recv.at[r],
+            {"chan": far if k else other, "src": core},
+        )
+
+    for r in range(PARTS):
+
+        @pl.when(tm > 0)
+        def _():
+            to_after(r).start()
+
+        @pl.when(tm < ntm - 1)
+        def _():
+            to_prev(r).start()
+
+    line = lax.broadcasted_iota(jnp.int32, (pairs, 128), 0)
+    own_names = jnp.zeros((pairs, 128), jnp.int32)
+    for p in range(pairs):
+        own_names = jnp.where(line == p, owner_ref[p] * targets + sub_ref[p], own_names)
+    names[0] = own_names.astype(jnp.float32)
+    line = lax.broadcasted_iota(jnp.int32, out_label.shape[1:], 0)
+    for k in range(nsrc):
+        owner = outer * nsrc + k
+        count = 0
+        found = [-1] * cap
+        for p in range(pairs):
+            hit = owner_ref[p] == owner
+            found = [jnp.where(jnp.logical_and(hit, count == j), p, found[j]) for j in range(cap)]
+            count = count + jnp.where(hit, 1, 0)
+        labels = jnp.full(out_label.shape[1:], -1, jnp.int32)
+        for j in range(cap):
+            pair = jnp.maximum(found[j], 0)
+            slot_pair[k * cap + j] = pair
+            name = jnp.where(found[j] >= 0, owner * targets + sub_ref[pair], -1)
+            labels = jnp.where(line == j, name, labels)
+        out_label[k] = labels.astype(jnp.float32)
+
+    name_to(1, {"src": mate}).start()
+
+    @pl.when(ending)
+    def _():
+        name_to(2, {"chan": inner, "src": core}).start()
+        name_to(3, {"chan": inner, "src": mate}).start()
+
+    @pl.when(middle)
+    def _():
+        for k in range(nsrc):
+            label_to(k, core).start()
+
+    for g in range(blocks):
+        tab[g] = jnp.broadcast_to(table_ref[g : g + 1, :], (block_rows, block_rows)).T
+
+    name_to(1, {"src": mate}).wait_recv()
+
+    @pl.when(middle)
+    def _():
+        name_to(2, {"chan": inner, "src": core}).wait_recv()
+        name_to(3, {"chan": inner, "src": mate}).wait_recv()
+
+    @pl.when(ending)
+    def _():
+        for k in range(nsrc):
+            label_to(k, k).wait_recv()
+
+    def produce(r):
+        @pl.when(tm > 0)
+        def _():
+            to_prev(r).wait_recv()
+
+        @pl.when(tm < ntm - 1)
+        def _():
+            to_after(r).wait_recv()
+
+        window = jnp.concatenate(
+            [
+                prev[:, part(r), :].reshape(rows, ntaps),
+                record[:, part(r), :].reshape(rows, seg),
+                after[:, part(r), :].reshape(rows, seg),
+            ],
+            axis=1,
+        )
+        inside = jnp.where(tm < ntm - 1, 1.0, 0.0)
+        which = tab[:, part(r), :].reshape(rows, block_rows)
+        band_filter(window, band_hi, band_lo, which, inside, seg, ntab, filt)
+
+        def one_pair(p, c):
+            value = shift_pair(filt[block_ref[p]], delay_ref[p], frac_ref[p], seg)
+            held[p, part(r), :] = value
+            shifted[p] = value
+            return c
+
+        lax.fori_loop(0, pairs, one_pair, 0, unroll=min(pairs, 4))
+        held_to(1, r, {"src": mate}).start()
+
+        @pl.when(ending)
+        def _():
+            held_to(2, r, {"chan": inner, "src": core}).start()
+
+        @pl.when(middle)
+        def _():
+            for k in range(nsrc):
+                for j in range(cap):
+                    out_slots[k, j, part(r), :] = shifted[slot_pair[k * cap + j]]
+                slots_to(k, r, core).start()
+
+    def relay(r):
+        held_to(2, r, {"chan": inner, "src": core}).wait_recv()
+        held_to(3, r, {"src": mate}).start()
+
+    def summed(r, first_names, kinds, depth):
+        def one_kind(kind, running):
+            total = list(running)
+            for p in range(pairs):
+                value = held[kind * pairs + p, part(r), :].astype(jnp.float32)
+                name = names[kind, p : p + 1, :]
+                name = jnp.concatenate([name] * (seg // 128), axis=1)
+                for b in range(depth):
+                    hit = name == first_names[b]
+                    total[b] = total[b] + jnp.where(hit, value, 0.0)
+            return tuple(total)
+
+        empty = jnp.zeros((step_rows, seg), jnp.float32)
+        return lax.fori_loop(0, kinds, one_kind, (empty,) * depth)
+
+    def names_of(chan):
+        start = (chan * nsrc + core) * targets
+        return [(start + b).astype(jnp.float32) for b in range(targets)]
+
+    def dense(r):
+        held_to(1, r, {"src": mate}).wait_recv()
+        held_to(3, r, {"src": mate}).wait_recv()
+        wanted = names_of(far) + names_of(other)
+        total = summed(r, wanted, 4, 2 * targets)
+        for k, base in ((1, 0), (0, targets)):
+            for b in range(targets):
+                out_dense[k, b, part(r), :] = total[base + b].astype(jnp.bfloat16)
+            dense_to(k, r).start()
+
+    def produce_step(i, carry):
+        @pl.when(i < PARTS)
+        def _():
+            produce(i)
+
+        @pl.when(jnp.logical_and(middle, jnp.logical_and(i >= LAG, i < PARTS + LAG)))
+        def _():
+            relay(i - LAG)
+
+        @pl.when(jnp.logical_and(middle, i >= LAG + MORE))
+        def _():
+            dense(i - LAG - MORE)
+
+        return carry
+
+    lax.fori_loop(0, PARTS + LAG + MORE, produce_step, 0)
+
+    def finish(r, carry):
+        @pl.when(ending)
+        def _():
+            held_to(1, r, {"src": mate}).wait_recv()
+
+        mine = names_of(chip)
+        total = summed(r, mine, jnp.where(middle, 4, 2), targets)
+        for b in range(targets):
+            sums[b, part(r), :] = total[b]
+
+        @pl.when(ending)
+        def _():
+            total = [sums[b, part(r), :] for b in range(targets)]
+            for k in range(nsrc):
+                slots_to(k, r, k).wait_recv()
+                for j in range(cap):
+                    value = in_slots[k, j, part(r), :].astype(jnp.float32)
+                    name = in_label[k, j : j + 1, :]
+                    name = jnp.concatenate([name] * (seg // 128), axis=1)
+                    total = [
+                        total[b] + jnp.where(name == mine[b], value, 0.0) for b in range(targets)
+                    ]
+            for b in range(targets):
+                sums[b, part(r), :] = total[b]
+
+        dense_to(0, r).wait_recv()
+        for b in range(targets):
+            sums[b, part(r), :] = sums[b, part(r), :] + in_dense[b, part(r), :].astype(jnp.float32)
+        return carry
+
+    lax.fori_loop(0, PARTS, finish, 0)
+
+    for b in range(targets):
+        high, low = split(sums[b])
+        beam_ref[b * points : (b + 1) * points, :] = mm(steer_ref[b], high) + mm(steer_ref[b], low)
+
+    name_to(1, {"src": mate}).wait_send()
+
+    @pl.when(ending)
+    def _():
+        name_to(2, {"chan": inner, "src": core}).wait_send()
+        name_to(3, {"chan": inner, "src": mate}).wait_send()
+
+    @pl.when(middle)
+    def _():
+        for k in range(nsrc):
+            label_to(k, core).wait_send()
+
+    def leave(r, carry):
+        @pl.when(tm > 0)
+        def _():
+            to_after(r).wait_send()
+
+        @pl.when(tm < ntm - 1)
+        def _():
+            to_prev(r).wait_send()
+
+        held_to(1, r, {"src": mate}).wait_send()
+
+        @pl.when(ending)
+        def _():
+            held_to(2, r, {"chan": inner, "src": core}).wait_send()
+
+        @pl.when(middle)
+        def _():
+            held_to(3, r, {"src": mate}).wait_send()
+            for k in range(nsrc):
+                slots_to(k, r, core).wait_send()
+            for k in range(2):
+                dense_to(k, r).wait_send()
+
+        return carry
+
+    lax.fori_loop(0, PARTS, leave, 0)
+
+
+def build_band(taps_ref, band_hi, band_lo):
+    ntab, ntaps = taps_ref.shape
+    for m in range(ntab):
+        row = jnp.concatenate([taps_ref[m : m + 1, :], jnp.zeros((1, ntaps), jnp.float32)], axis=1)
+        full = jnp.broadcast_to(row, (2 * ntaps, 2 * ntaps))
+        rolled = pltpu.roll(full, ntaps, 1, stride=1, stride_axis=0)[:, :ntaps]
+        high, low = split(rolled)
+        band_hi[:, m * ntaps : (m + 1) * ntaps] = high
+        band_lo[:, m * ntaps : (m + 1) * ntaps] = low
+
+
+def band_filter(window, band_hi, band_lo, which, inside, seg, ntab, filt):
+    blocks, step_rows, _ = filt.shape
+    rows = blocks * step_rows
+    ntaps = band_hi.shape[0] // 2
+    high, low = split(window)
+    steps = 2 * seg // ntaps
+    lhs_hi = jnp.concatenate([high[:, j * ntaps : (j + 2) * ntaps] for j in range(steps)], axis=0)
+    lhs_lo = jnp.concatenate([low[:, j * ntaps : (j + 2) * ntaps] for j in range(steps)], axis=0)
+    every = mm(lhs_lo, band_hi[...]) + mm(lhs_hi, band_lo[...]) + mm(lhs_hi, band_hi[...])
+    for j in range(steps):
+        own = every[j * rows : (j + 1) * rows]
+        value = own[:, :ntaps]
+        for m in range(1, ntab):
+            value = jnp.where(which == m, own[:, m * ntaps : (m + 1) * ntaps], value)
+        if j >= seg // ntaps:
+            value = value * inside
+        filt[:, :, j * ntaps : (j + 1) * ntaps] = value.reshape(blocks, step_rows, ntaps)
+
+
+def shift_pair(source, delay, frac, seg):
+    mu = jnp.full((1, seg), frac.astype(jnp.float32)) / NFRAC
+    first = -mu * (mu - 1.0) * (mu - 2.0) / 6.0
+    second = (mu + 1.0) * (mu - 1.0) * (mu - 2.0) / 2.0
+    third = -(mu + 1.0) * mu * (mu - 2.0) / 2.0
+    fourth = (mu + 1.0) * mu * (mu - 1.0) / 6.0
+    base = pltpu.roll(source, 2 * seg - (delay - 1), 1)
+    mixed = first * base[:, :seg]
+    mixed = mixed + second * pltpu.roll(base, 2 * seg - 1, 1)[:, :seg]
+    mixed = mixed + third * pltpu.roll(base, 2 * seg - 2, 1)[:, :seg]
+    mixed = mixed + fourth * pltpu.roll(base, 2 * seg - 3, 1)[:, :seg]
+    return mixed.astype(jnp.bfloat16)
 
 
 def solution(mesh):
@@ -332,6 +759,58 @@
         smem = pl.BlockSpec(memory_space=pltpu.SMEM)
         vmem = pl.BlockSpec(memory_space=pltpu.VMEM)
         dma = pltpu.SemaphoreType.DMA
+        operands = (
+            pair_block,
+            pair_owner.reshape(pairs),
+            pair_sub,
+            pair_delay,
+            pair_frac,
+            record.reshape(blocks, block_rows, seg),
+            fir_taps,
+            chan_table.reshape(blocks, block_rows),
+            steering,
+        )
+        if nchan == 4 and nsrc == 2:
+            return pl.pallas_call(
+                functools.partial(line_kernel, (nchan, nsrc, ntm)),
+                out_shape=jax.ShapeDtypeStruct((targets * points, seg), jnp.float32),
+                in_specs=[smem] * 5 + [vmem] * 4,
+                out_specs=vmem,
+                scratch_shapes=[
+                    pltpu.VMEM((blocks, block_rows, ntaps), jnp.float32),
+                    pltpu.VMEM((blocks, block_rows, seg), jnp.float32),
+                    pltpu.VMEM((2 * ntaps, ntab * ntaps), jnp.bfloat16),
+                    pltpu.VMEM((2 * ntaps, ntab * ntaps), jnp.bfloat16),
+                    pltpu.VMEM((blocks, block_rows, block_rows), jnp.int32),
+                    pltpu.VMEM((blocks, block_rows // PARTS, 2 * seg), jnp.float32),
+                    pltpu.VMEM((pairs, block_rows // PARTS, seg), jnp.bfloat16),
+                    pltpu.VMEM((4 * pairs, block_rows, seg), jnp.bfloat16),
+                    pltpu.VMEM((4, pairs, 128), jnp.float32),
+                    pltpu.VMEM((nsrc, cap, block_rows, seg), jnp.bfloat16),
+                    pltpu.VMEM((nsrc, cap, block_rows, seg), jnp.bfloat16),
+                    pltpu.VMEM((nsrc, 8, 128), jnp.float32),
+                    pltpu.VMEM((nsrc, 8, 128), jnp.float32),
+                    pltpu.VMEM((2, targets, block_rows, seg), jnp.bfloat16),
+                    pltpu.VMEM((targets, block_rows, seg), jnp.bfloat16),
+                    pltpu.VMEM((targets, block_rows, seg), jnp.float32),
+                    pltpu.SMEM((nsrc * cap,), jnp.int32),
+                    dma((PARTS,)),
+                    dma((PARTS,)),
+                    dma((PARTS,)),
+                    dma((PARTS,)),
+                    dma((4, PARTS)),
+                    dma((4, PARTS)),
+                    dma((4,)),
+                    dma((4,)),
+                    dma((nsrc, PARTS)),
+                    dma((nsrc, PARTS)),
+                    dma((nsrc,)),
+                    dma((nsrc,)),
+                    dma((2, PARTS)),
+                    dma((PARTS,)),
+                ],
+                compiler_params=pltpu.CompilerParams(collective_id=0, has_side_effects=True),
+            )(*operands)
         return pl.pallas_call(
             functools.partial(kernel, (nchan, nsrc, ntm)),
             out_shape=jax.ShapeDtypeStruct((targets * points, seg), jnp.float32),
@@ -361,17 +840,7 @@
                 dma((owners,)),
             ],
             compiler_params=pltpu.CompilerParams(collective_id=0, has_side_effects=True),
-        )(
-            pair_block,
-            pair_owner.reshape(pairs),
-            pair_sub,
-            pair_delay,
-            pair_frac,
-            record.reshape(blocks, block_rows, seg),
-            fir_taps,
-            chan_table.reshape(blocks, block_rows),
-            steering,
-        )
+        )(*operands)
 
     in_specs = (
         P(("groups", "chan", "src"), "tm"),

time: 40.6 us -> 34 us (0.84)
  Pallas kernels: 38.1 us -> 31.6 us
    pallas_call x1, Pallas kernels: 38.1 us -> 31.6 us  [local(): pl.pallas_call(functools.partial(line_kernel, (nchan, nsrc, ntm)), out_sh...]
where the time goes in v2:
time: 34 us; the launch traced here: 33.9 us
  Pallas kernels  31.6 us (93%)
  local copies, waits for them, and re-layouts  2.26 us (7%)
    pallas_call x1, Pallas kernels, local(): pl.pallas_call(functools.partial(line_kernel, (nchan, nsrc, ntm)), out_sh...  31.6 us
    unnamed x1, local copies, waits for them, and re-layouts  2.26 us

profile of v2, /device:TPU:0, one launch (start us, length us, event | category | flops | bytes accessed | tf_op | source)
XLA Modules:
  0.0 33.9 jit_solution(1482515218524171131)
XLA Ops:
  0.0 31.6 %shard_map.91 = f32[1024,256]{1,0:T(8,128)} custom-call(s32[8]{0:T(128)} %block_ref.1, s32[8]{0:T(128)} %bitcast.5, s32[8]{0:T(128)} %sub_ref.1, s32[8]{0:T(128)} %delay_ref.1, s32[8]{0:T(128)} %frac_ref.1, f32[4,128,256]{2,1,0:T(8,128)} %bitcast.3, f32[4,128]{1,0:T(4,128)} %taps_ref.1, s32[4,128]{1,0:T(4,128)} %bitcast.4, bf16[4,256,128]{2,1,0:T(8,128)(2,1)} %steer_ref.1), custom_call_target="tpu_custom_call" | custom-call | tf_op jit(solution)/shard_map/pallas_call | solution.py:774
  31.6 2.3 %copy.11 = f32[1024,256]{1,0:T(8,128)} copy(f32[1024,256]{1,0:T(8,128)} %shard_map.91) | data formatting | bytes 2097152

commit v3 on v2

--- a/solution.py
+++ b/solution.py
@@ -310,8 +310,7 @@
     record,
     taps_ref,
     table_ref,
-    steer_ref,
-    beam_ref,
+    sums,
     prev,
     after,
     band_hi,
@@ -327,7 +326,6 @@
     in_label,
     out_dense,
     in_dense,
-    sums,
     slot_pair,
     prev_send,
     prev_recv,
@@ -349,8 +347,7 @@
     ntab, ntaps = taps_ref.shape
     pairs = block_ref.shape[0]
     cap = out_slots.shape[1]
-    targets = steer_ref.shape[0]
-    points = steer_ref.shape[1]
+    targets = sums.shape[0]
     step_rows = block_rows // PARTS
     rows = blocks * step_rows
     chip = lax.axis_index("chan")
@@ -653,10 +650,6 @@
         return carry
 
     lax.fori_loop(0, PARTS, finish, 0)
-
-    for b in range(targets):
-        high, low = split(sums[b])
-        beam_ref[b * points : (b + 1) * points, :] = mm(steer_ref[b], high) + mm(steer_ref[b], low)
 
     name_to(1, {"src": mate}).wait_send()
 
@@ -771,10 +764,10 @@
             steering,
         )
         if nchan == 4 and nsrc == 2:
-            return pl.pallas_call(
+            sums = pl.pallas_call(
                 functools.partial(line_kernel, (nchan, nsrc, ntm)),
-                out_shape=jax.ShapeDtypeStruct((targets * points, seg), jnp.float32),
-                in_specs=[smem] * 5 + [vmem] * 4,
+                out_shape=jax.ShapeDtypeStruct((targets, block_rows, seg), jnp.float32),
+                in_specs=[smem] * 5 + [vmem] * 3,
                 out_specs=vmem,
                 scratch_shapes=[
                     pltpu.VMEM((blocks, block_rows, ntaps), jnp.float32),
@@ -792,7 +785,6 @@
                     pltpu.VMEM((nsrc, 8, 128), jnp.float32),
                     pltpu.VMEM((2, targets, block_rows, seg), jnp.bfloat16),
                     pltpu.VMEM((targets, block_rows, seg), jnp.bfloat16),
-                    pltpu.VMEM((targets, block_rows, seg), jnp.float32),
                     pltpu.SMEM((nsrc * cap,), jnp.int32),
                     dma((PARTS,)),
                     dma((PARTS,)),
@@ -810,7 +802,14 @@
                     dma((PARTS,)),
                 ],
                 compiler_params=pltpu.CompilerParams(collective_id=0, has_side_effects=True),
-            )(*operands)
+            )(*operands[:-1])
+            beam = jnp.einsum(
+                "bxc,bct->bxt",
+                steering.astype(jnp.float32),
+                sums,
+                precision=lax.Precision.HIGHEST,
+            )
+            return beam.reshape(targets * points, seg)
         return pl.pallas_call(
             functools.partial(kernel, (nchan, nsrc, ntm)),
             out_shape=jax.ShapeDtypeStruct((targets * points, seg), jnp.float32),

time: 34 us -> 33.7 us (level)
  matrix products: 0 us -> 2.61 us
  local copies, waits for them, and re-layouts: 2.26 us -> 0.01 us
  Pallas kernels: 31.6 us -> 30.9 us
    dot_general x0 -> x1, matrix products: none -> 2.61 us  [local(): jnp.einsum('bxc,bct->bxt', steering.astype(jnp.float32), sums, precision=...]
    unnamed x1 -> x2, local copies, waits for them, and re-layouts: 2.26 us -> 0.01 us
    pallas_call x1, Pallas kernels: 31.6 us -> 30.9 us  [local(): pl.pallas_call(functools.partial(line_kernel, (nchan, nsrc, ntm)), out_sh...]
where the time goes in v3:
time: 33.7 us; the launch traced here: 33.5 us
  Pallas kernels  30.9 us (92%)
  matrix products  2.61 us (8%)
    pallas_call x1, Pallas kernels, local(): pl.pallas_call(functools.partial(line_kernel, (nchan, nsrc, ntm)), out_sh...  30.9 us
    dot_general x1, matrix products, local(): jnp.einsum('bxc,bct->bxt', steering.astype(jnp.float32), sums, precision=...  2.61 us

profile of v3, /device:TPU:0, one launch (start us, length us, event | category | flops | bytes accessed | tf_op | source)
XLA Modules:
  0.0 33.5 jit_solution(8403224527974136391)
XLA Ops:
  0.0 0.0 copy-start
  0.0 30.9 %shard_map.91 = f32[4,128,256]{2,1,0:T(8,128)} custom-call(s32[8]{0:T(128)} %block_ref.1, s32[8]{0:T(128)} %bitcast.10, s32[8]{0:T(128)} %sub_ref.1, s32[8]{0:T(128)} %delay_ref.1, s32[8]{0:T(128)} %frac_ref.1, f32[4,128,256]{2,1,0:T(8,128)} %bitcast.8, f32[4,128]{1,0:T(4,128)} %taps_ref.1, s32[4,128]{1,0:T(4,128)} %bitcast.9), custom_call_target="tpu_custom_call" | custom-call | tf_op jit(solution)/shard_map/pallas_call | solution.py:767
  30.9 0.0 copy-done
  30.9 2.6 %fusion = f32[4,256,256]{1,2,0:T(8,128)} fusion(f32[4,128,256]{2,1,0:T(8,128)} %shard_map.91, bf16[4,256,128]{2,1,0:T(8,128)(2,1)S(1)} %copy-done), kind=kOutput, calls=%fused_computation | convolution fusion | flops 402653184 | bytes 1835008 | tf_op jit(solution)/shard_map/bxc,bct->bxt/dot_general | solution.py:806
Async XLA Ops:
  0.0 30.9 %copy-start = (bf16[4,256,128]{2,1,0:T(8,128)(2,1)S(1)}, bf16[4,256,128]{2,1,0:T(8,128)(2,1)}, u32[]{:S(2)}) copy-start(bf16[4,256,128]{2,1,0:T(8,128)(2,1)} %param.12) | copy-start | bytes 786436
